TPU v7x, 32 devices: a whole 2x2x4 slice. The times are simulated.
32 devices in a mesh: row: 4 (over z), col: 8 (over y, x, core).
Axes of the slice: x: 2, y: 2, z: 4, core: 2. Of those that a mesh axis runs over, the one named last changes fastest.
Arguments:
- amplitudes: bfloat16 [2048, 8192], P(('col', 'row')), may hold values from -6 to 6
- integrals: bfloat16 [8192, 8192], P('row', 'col'), may hold values from -0.0625 to 0.0625
- integral_tiles: int32 [64, 64], P('row', 'col'), may hold values from 0 to 1, as said below
- amplitude_tiles: int32 [16, 64], P('col'), may hold values 0 or 1
Outputs:
- ladder: float32 [2048, 8192], P('col', 'row')
Inputs may be any that keep to these rules, and one draw needn't show every extreme that they name: `integral_tiles`: tiles of higher ab index are more often nonzero.
All inputs are finite; a program needn't handle non-finite values. No bound on the sum of `amplitude_tiles` on one device may be relied on, other than what follows from the above.
Results may differ from a plain program's by a relative error of at most 0.0003.
Values may be sent and summed in bfloat16 or wider, within the bound.
No kernel may reach another device: no remote copies, remote signals or barrier semaphores. Data moves between devices by JAX's collectives and lax.ppermute only.
A program may use at most 128 MiB of HBM per device.

v0:
```python
import jax
import jax.numpy as jnp
from jax import lax
from jax.sharding import PartitionSpec as P

TILE = 128


def contract(left, right):
    return lax.dot_general(
        left, right, (((1,), (1,)), ((), ())), preferred_element_type=jnp.float32
    )


def on_device(amplitudes, integrals, integral_tiles, amplitude_tiles):
    local_rows = amplitudes.shape[0]
    tile_rows = jnp.repeat(amplitude_tiles, TILE, axis=0)
    tile_rows = lax.dynamic_slice_in_dim(
        tile_rows, lax.axis_index("row") * local_rows, local_rows, 0
    )
    amp_mask = jnp.repeat(tile_rows, TILE, axis=1).astype(jnp.bfloat16)
    masked_amps = amplitudes * amp_mask
    int_mask = jnp.repeat(jnp.repeat(integral_tiles, TILE, axis=0), TILE, axis=1).astype(
        jnp.bfloat16
    )
    masked_ints = integrals * int_mask
    panel = lax.all_gather(masked_amps, "row", axis=0, tiled=True)
    return contract(panel, lax.all_gather(masked_ints, "col", axis=1, tiled=True))


def solution(mesh):
    return jax.shard_map(
        on_device,
        mesh=mesh,
        in_specs=(P(("col", "row"), None), P("row", "col"), P("row", "col"), P("col", None)),
        out_specs=P("col", "row"),
        check_vma=False,
    )
```

profile of v0, /device:TPU:0, one launch (start us, length us, event | category | flops | bytes accessed | tf_op | source)
XLA Modules:
  0.0 279.3 jit_solution(6280737660417096425)
XLA Ops:
  6.5 0.0 copy-start.1
  6.5 0.0 all-gather.3.cloned.1.call-start
  6.5 0.7 broadcast_in_dim.12
  7.3 0.6 broadcast_in_dim.13
  7.9 2.8 %bitcast_multiply_fusion.1 = bf16[64,8192]{1,0:T(8,128)(2,1)} fusion(bf16[64,8192]{1,0:T(8,128)(2,1)} %param.4, bf16[8,8,64,128]{3,2,1,0:T(8,128)(2,1)S(1)} %bitcast.11), kind=kLoop, calls=%fused_computation.1 | loop fusion | flops 524288 | bytes 3145728 | tf_op jit(solution)/shard_map/mul | solution.py:22
  10.7 0.0 all-gather.3.cloned.1.call-update
  10.7 0.0 all-gather.5.cloned.1.call-start
  10.8 0.0 copy-done.1
  10.8 0.1 copy.5
  10.9 0.0 copy-start
  10.9 0.1 broadcast_in_dim.14
  11.0 5.8 %broadcast_in_dim.15 = bf16[2048,8,128]{2,1,0:T(8,128)(2,1)S(1)} broadcast(bf16[2048,8]{1,0:T(8,128)(2,1)S(1)} %bitcast.12), dimensions={0,1} | broadcast | bytes 4227072 | tf_op jit(solution)/shard_map/broadcast_in_dim | solution.py:23
  16.8 0.0 copy-done
  16.8 2.5 bitcast_multiply_fusion
  19.3 0.0 all-gather.5.cloned.1.call-update
  19.3 75.1 %all-gather.3.cloned.1.call-done = bf16[256,8192]{1,0:T(8,128)(2,1)} async-done(((bf16[64,8192]{1,0:T(8,128)(2,1)}), bf16[256,8192]{1,0:T(8,128)(2,1)}) %all-gather.3.cloned.1.call-update) | async-done | bytes 4194320 | tf_op jit(solution)/shard_map/all_gather | solution.py:27
  94.3 161.3 %all-gather.5.cloned.1.call-done = bf16[2048,8192]{1,0:T(8,128)(2,1)} async-done(((bf16[2048,1024]{1,0:T(8,128)(2,1)}), bf16[2048,8192]{1,0:T(8,128)(2,1)}) %all-gather.5.cloned.1.call-update) | async-done | bytes 33554448 | tf_op jit(solution)/shard_map/all_gather | solution.py:28
  255.6 16.9 %fusion = f32[256,2048]{1,0:T(8,128)} fusion(bf16[256,8192]{1,0:T(8,128)(2,1)} %all-gather.3.cloned.1.call-done, bf16[2048,8192]{1,0:T(8,128)(2,1)} %all-gather.5.cloned.1.call-done), kind=kOutput, calls=%fused_computation.3 | convolution fusion | flops 8589934592 | bytes 39845888 | tf_op jit(solution)/shard_map/dot_general | solution.py:10
  (2 shorter events, 0.0 us)
Async XLA Ops:
  6.5 4.2 %copy-start.1 = (s32[16,8]{0,1:T(8,128)S(1)}, s32[16,8]{0,1:T(8,128)}, u32[]{:S(2)}) copy-start(s32[16,8]{0,1:T(8,128)} %param.6) | copy-start | bytes 1540
  6.5 87.8 %all-gather.3.cloned.1.call-start = ((), (), s32[]{:S(2)}) async-start(), calls=%async_computation | async-start | bytes 5242880 | tf_op jit(solution)/shard_map/all_gather | solution.py:27
  10.7 244.9 %all-gather.5.cloned.1.call-start = ((), (), s32[]{:S(2)}) async-start(), calls=%async_computation.1 | async-start | bytes 37748736 | tf_op jit(solution)/shard_map/all_gather | solution.py:28
  10.9 5.9 %copy-start = (bf16[2048,1024]{1,0:T(8,128)(2,1)S(1)}, bf16[2048,1024]{1,0:T(8,128)(2,1)}, u32[]{:S(2)}) copy-start(bf16[2048,1024]{1,0:T(8,128)(2,1)} %param.5) | copy-start | bytes 12582916
Sparse Core Ops, SparseCore 0:
  10.8 83.4 all-gather.2
  96.2 159.3 all-gather.4
where the time goes:
time: 280 us; the launch traced here: 279 us
  waiting for transfers between devices  236 us (84%)
  matrix products  16.9 us (6%)
  between operations  13.5 us (5%)
  local copies, waits for them, and re-layouts  7.25 us (3%)
  other arithmetic  5.35 us (2%)
    all_gather x1, waiting for transfers between devices, on_device(): lax.all_gather(masked_ints, 'col', axis=1, tiled=True)  161 us
    all_gather x1, waiting for transfers between devices, on_device(): panel = lax.all_gather(masked_amps, 'row', axis=0, tiled=True)  75.1 us
    dot_general x1, matrix products, contract(): lax.dot_general(left, right, (((1,), (1,)), ((), ())), preferred_element_...  16.9 us
    broadcast_in_dim x1, local copies, waits for them, and re-layouts, on_device(): jnp.repeat(jnp.repeat(integral_tiles, TILE, axis=0), TILE, axis=1)  5.78 us
  transfers between devices with their start and end apart: 2, of which 2 were waited for; matrix products, arithmetic and copies ran while one was open for 3% of the time, Pallas kernels for 0%

commit v1 on v0

--- a/solution.py
+++ b/solution.py
@@ -24,7 +24,16 @@
         jnp.bfloat16
     )
     masked_ints = integrals * int_mask
-    panel = lax.all_gather(masked_amps, "row", axis=0, tiled=True)
+    ways = lax.axis_size("row")
+    up = [(d, (d + 1) % ways) for d in range(ways)]
+    down = [(d, (d - 1) % ways) for d in range(ways)]
+    earlier, later = ([masked_amps], [masked_amps])
+    for _ in range(ways // 2):
+        earlier.append(lax.ppermute(earlier[-1], "row", up))
+    for _ in range((ways - 1) // 2):
+        later.append(lax.ppermute(later[-1], "row", down))
+    line = jnp.concatenate([*earlier[::-1], *later[1:]], axis=0)
+    panel = jnp.roll(line, (lax.axis_index("row") - ways // 2) * masked_amps.shape[0], axis=0)
     return contract(panel, lax.all_gather(masked_ints, "col", axis=1, tiled=True))
 
 

time: 280 us -> 206 us (0.74)
  waiting for transfers between devices: 236 us -> 144 us
  local copies, waits for them, and re-layouts: 7.25 us -> 17.5 us
  starting transfers between devices: 0.04 us -> 6.9 us
    all_gather x1, waiting for transfers between devices: 161 us -> 80.7 us  [on_device(): lax.all_gather(masked_ints, 'col', axis=1, tiled=True)]
    all_gather x1 -> x0, waiting for transfers between devices: 75.1 us -> none  [on_device(): panel = lax.all_gather(masked_amps, 'row', axis=0, tiled=True)]
    ppermute x0 -> x3, waiting for transfers between devices: none -> 63.8 us  [the longest x2 49.4 us: on_device(): earlier.append(lax.ppermute(earlier[-1], 'row', up))]
    unnamed x4 -> x11, local copies, waits for them, and re-layouts: 0.01 us -> 9.86 us
    ppermute x0 -> x3, starting transfers between devices: none -> 6.9 us  [the longest x1 3.82 us: on_device(): later.append(lax.ppermute(later[-1], 'row', down))]
  transfers between devices with their start and end apart: 2 -> 4, of which waited for: 2 -> 4; matrix products, arithmetic and copies ran while one was open for 3% -> 6% of each run, Pallas kernels for 0% -> 0%
where the time goes in v1:
time: 206 us; the launch traced here: 205 us
  waiting for transfers between devices  144 us (70%)
  local copies, waits for them, and re-layouts  17.5 us (8%)
  matrix products  16.9 us (8%)
  between operations  13.5 us (7%)
  starting transfers between devices  6.9 us (3%)
  other arithmetic  6.14 us (3%)
    all_gather x1, waiting for transfers between devices, on_device(): lax.all_gather(masked_ints, 'col', axis=1, tiled=True)  80.7 us
    ppermute x2, waiting for transfers between devices, on_device(): earlier.append(lax.ppermute(earlier[-1], 'row', up))  49.4 us
    dot_general x1, matrix products, contract(): lax.dot_general(left, right, (((1,), (1,)), ((), ())), preferred_element_...  16.9 us
    ppermute x1, waiting for transfers between devices, on_device(): later.append(lax.ppermute(later[-1], 'row', down))  14.4 us
    unnamed x11, local copies, waits for them, and re-layouts  9.86 us
    broadcast_in_dim x1, local copies, waits for them, and re-layouts, on_device(): jnp.repeat(jnp.repeat(integral_tiles, TILE, axis=0), TILE, axis=1)  5.78 us
    mul x1, other arithmetic, on_device(): masked_ints = integrals * int_mask  4.75 us
  transfers between devices with their start and end apart: 4, of which 4 were waited for; matrix products, arithmetic and copies ran while one was open for 6% of the time, Pallas kernels for 0%

profile of v1, /device:TPU:0, one launch (start us, length us, event | category | flops | bytes accessed | tf_op | source)
XLA Modules:
  0.0 205.4 jit_solution(5551393202494412385)
XLA Ops:
  6.5 0.7 convert_element_type.20
  7.2 0.1 copy.5
  7.3 0.1 broadcast_in_dim.14
  7.4 5.8 %broadcast_in_dim.15 = bf16[2048,8,128]{2,1,0:T(8,128)(2,1)S(1)} broadcast(bf16[2048,8]{1,0:T(8,128)(2,1)S(1)} %bitcast.11), dimensions={0,1} | broadcast | bytes 4227072 | tf_op jit(solution)/shard_map/broadcast_in_dim | solution.py:23
  13.2 0.0 copy-start.1
  13.2 4.8 %bitcast_multiply_fusion = bf16[2048,1024]{1,0:T(8,128)(2,1)} fusion(bf16[2048,1024]{1,0:T(8,128)(2,1)} %param.5, bf16[256,8,8,128]{3,2,1,0:T(8,128)(2,1)S(1)} %bitcast.9), kind=kLoop, calls=%fused_computation | loop fusion | flops 2097152 | bytes 12582912 | tf_op jit(solution)/shard_map/mul | solution.py:26
  18.0 0.0 all-gather.2.cloned.1.call-update
  18.0 0.6 broadcast_in_dim.13
  18.7 0.7 bitcast_multiply_fusion.1
  19.4 3.1 %collective-permute-start = (bf16[64,8192]{1,0:T(8,128)(2,1)S(1)}, bf16[64,8192]{1,0:T(8,128)(2,1)S(1)}, u32[]{:S(2)}, u32[]{:S(2)}) collective-permute-start(bf16[64,8192]{1,0:T(8,128)(2,1)S(1)} %bitcast_multiply_fusion.1), channel_id=1, source_target_pairs={{0,8},{8,16},{16,24},{24,0},{1,9},{9,17},{17,25},{25,1},{2,10},{10... | collective-permute-start | bytes 3145736 | tf_op jit(solution)/shard_map/ppermute | solution.py:32
  22.4 25.2 %collective-permute-done = bf16[64,8192]{1,0:T(8,128)(2,1)S(1)} collective-permute-done((bf16[64,8192]{1,0:T(8,128)(2,1)S(1)}, bf16[64,8192]{1,0:T(8,128)(2,1)S(1)}, u32[]{:S(2)}, u32[]{:S(2)}) %collective-permute-start) | collective-permute-done | bytes 1048608 | tf_op jit(solution)/shard_map/ppermute | solution.py:32
  47.6 3.8 %collective-permute-start.2 = (bf16[64,8192]{1,0:T(8,128)(2,1)S(1)}, bf16[64,8192]{1,0:T(8,128)(2,1)S(1)}, u32[]{:S(2)}, u32[]{:S(2)}) collective-permute-start(bf16[64,8192]{1,0:T(8,128)(2,1)S(1)} %bitcast_multiply_fusion.1), channel_id=1, source_target_pairs={{0,24},{8,0},{16,8},{24,16},{1,25},{9,1},{17,9},{25,17},{2,26},{10... | collective-permute-start | bytes 3145736 | tf_op jit(solution)/shard_map/ppermute | solution.py:34
  51.4 24.2 %collective-permute-done.1 = bf16[64,8192]{1,0:T(8,128)(2,1)} collective-permute-done((bf16[64,8192]{1,0:T(8,128)(2,1)S(1)}, bf16[64,8192]{1,0:T(8,128)(2,1)}, u32[]{:S(2)}, u32[]{:S(2)}) %collective-permute-start.1) | collective-permute-done | bytes 1048608 | tf_op jit(solution)/shard_map/ppermute | solution.py:32
  75.6 2.3 %constant_dynamic-update-slice_fusion.7 = bf16[512,8192]{1,0:T(8,128)(2,1)} fusion(bf16[64,8192]{1,0:T(8,128)(2,1)} %collective-permute-done.1), kind=kLoop, calls=%fused_computation.12 | loop fusion | bytes 2097152
  77.9 1.1 constant_dynamic-update-slice_fusion.6
  79.0 1.0 constant_dynamic-update-slice_fusion.5
  80.0 14.4 %collective-permute-done.2 = bf16[64,8192]{1,0:T(8,128)(2,1)S(1)} collective-permute-done((bf16[64,8192]{1,0:T(8,128)(2,1)S(1)}, bf16[64,8192]{1,0:T(8,128)(2,1)S(1)}, u32[]{:S(2)}, u32[]{:S(2)}) %collective-permute-start.2) | collective-permute-done | bytes 1048608 | tf_op jit(solution)/shard_map/ppermute | solution.py:34
  94.4 1.1 constant_dynamic-update-slice_fusion.4
  95.5 2.3 %constant_dynamic-update-slice_fusion.3 = bf16[512,8192]{1,0:T(8,128)(2,1)} fusion(bf16[512,8192]{1,0:T(8,128)(2,1)} %constant_dynamic-update-slice_fusion.4, bf16[64,8192]{1,0:T(8,128)(2,1)} %collective-permute-done.1), kind=kLoop, calls=%fused_computation.8 | loop fusion | bytes 2097152
  97.8 1.0 constant_dynamic-update-slice_fusion.2
  98.8 1.1 constant_dynamic-update-slice_fusion.1
  99.9 1.1 constant_dynamic-update-slice_fusion
  101.0 80.7 %all-gather.2.cloned.1.call-done = bf16[2048,8192]{1,0:T(8,128)(2,1)} async-done(((bf16[2048,1024]{1,0:T(8,128)(2,1)}), bf16[2048,8192]{1,0:T(8,128)(2,1)}) %all-gather.2.cloned.1.call-update) | async-done | bytes 33554448 | tf_op jit(solution)/shard_map/all_gather | solution.py:37
  181.6 16.9 %fusion = f32[256,2048]{1,0:T(8,128)} fusion(bf16[2048,8192]{1,0:T(8,128)(2,1)} %all-gather.2.cloned.1.call-done, bf16[512,8192]{1,0:T(8,128)(2,1)} %constant_dynamic-update-slice_fusion, s32[]{:T(128)S(6)} %select_n.18), kind=kOutput, calls=%fused_computation.1 | convolution fusion | flops 8589934592 | bytes 39845892 | tf_op jit(solution)/shard_map/dot_general | solution.py:10
  (7 shorter events, 0.0 us)
Async XLA Ops:
  6.5 175.1 %all-gather.2.cloned.1.call-start = ((), (), s32[]{:S(2)}) async-start(), calls=%async_computation | async-start | bytes 37748736 | tf_op jit(solution)/shard_map/all_gather | solution.py:37
  13.2 4.8 %copy-start.1 = (s32[2,64]{1,0:T(2,128)S(1)}, s32[2,64]{1,0:T(2,128)}, u32[]{:S(2)}) copy-start(s32[2,64]{1,0:T(2,128)} %param.7) | copy-start | bytes 1540
  13.2 5.5 %copy-start = (bf16[64,8192]{1,0:T(8,128)(2,1)S(1)}, bf16[64,8192]{1,0:T(8,128)(2,1)}, u32[]{:S(2)}) copy-start(bf16[64,8192]{1,0:T(8,128)(2,1)} %param.4) | copy-start | bytes 3145732
  19.4 28.3 %collective-permute-start = (bf16[64,8192]{1,0:T(8,128)(2,1)S(1)}, bf16[64,8192]{1,0:T(8,128)(2,1)S(1)}, u32[]{:S(2)}, u32[]{:S(2)}) collective-permute-start(bf16[64,8192]{1,0:T(8,128)(2,1)S(1)} %bitcast_multiply_fusion.1), channel_id=1, source_target_pairs={{0,8},{8,16},{16,24},{24,0},{1,9},{9,17},{17,25},{25,1},{2,10},{10... | collective-permute-start | bytes 3145736 | tf_op jit(solution)/shard_map/ppermute | solution.py:32
  47.6 28.0 %collective-permute-start.1 = (bf16[64,8192]{1,0:T(8,128)(2,1)S(1)}, bf16[64,8192]{1,0:T(8,128)(2,1)}, u32[]{:S(2)}, u32[]{:S(2)}) collective-permute-start(bf16[64,8192]{1,0:T(8,128)(2,1)S(1)} %collective-permute-done), channel_id=1, source_target_pairs={{0,8},{8,16},{16,24},{24,0},{1,9},{9,17},{17,25},{25,1},{2,10},{10... | collective-permute-start | bytes 3145736 | tf_op jit(solution)/shard_map/ppermute | solution.py:32
  47.6 46.8 %collective-permute-start.2 = (bf16[64,8192]{1,0:T(8,128)(2,1)S(1)}, bf16[64,8192]{1,0:T(8,128)(2,1)S(1)}, u32[]{:S(2)}, u32[]{:S(2)}) collective-permute-start(bf16[64,8192]{1,0:T(8,128)(2,1)S(1)} %bitcast_multiply_fusion.1), channel_id=1, source_target_pairs={{0,24},{8,0},{16,8},{24,16},{1,25},{9,1},{17,9},{25,17},{2,26},{10... | collective-permute-start | bytes 3145736 | tf_op jit(solution)/shard_map/ppermute | solution.py:34
Sparse Core Ops, SparseCore 0:
  18.1 163.4 all-gather.1
